TPU v7x, 256 devices: a whole 4x4x8 slice. The times are simulated.
256 devices in a mesh: seq: 64 (over z, x, core), tp: 4 (over y).
Axes of the slice: x: 4, y: 4, z: 8, core: 2. Of those that a mesh axis runs over, the one named last changes fastest.
Arguments:
- hidden: bfloat16 [32768, 4096], P(('seq', 'tp')), may hold values from -640 to 640
- norm_gain: float32 [4096], replicated, may hold values from 0.5 to 1.5
- w_query: bfloat16 [4096, 2048], P(None, 'tp'), may hold values from -0.078125 to 0.078125
- w_key: bfloat16 [4096, 1024], P(None, 'tp'), may hold values from -2.421875 to 2.421875
- w_value: bfloat16 [4096, 1024], P(None, 'tp'), may hold values from -0.09375 to 0.09375
- doc_start: int32 [32768], P('seq'), may hold values from 0 to 32767, as said below
- block_owner: int32 [1024], P('seq'), may hold values from 0 to 63, as said below
Outputs:
- context_rows: bfloat16 [32768, 2048], P(('seq', 'tp'))
- key_cache: bfloat16 [49152, 1024], P('seq', 'tp')
- value_cache: bfloat16 [49152, 1024], P('seq', 'tp')
Inputs may be any that keep to these rules, and one draw needn't show every extreme that they name: `doc_start`: rows with equal values form one document: consecutive rows beginning at the row whose number is that value. Every document has at most 256 rows and one has exactly 256; all but the last have at least 64. `block_owner`: owner numbers never fall along the blocks. Owner o holds the blocks from o * 16 + e(o) up to (o + 1) * 16 + e(o + 1) - 1, where -4 <= e <= 4 and e is 0 at both ends of the axis; so an owner holds between 8 and 24 blocks, and some owner holds exactly 24.
All inputs are finite; a program needn't handle non-finite values.
Results may differ from a plain program's by a relative error of at most 0.0078.
Values may be sent and summed in bfloat16 or wider, within the bound.
No kernel may reach another device: no remote copies, remote signals or barrier semaphores. Data moves between devices by JAX's collectives and lax.ppermute only.
A program may use at most 128 MiB of HBM per device.

v0:
```python
import jax
import jax.numpy as jnp
from jax import lax
from jax.sharding import PartitionSpec as P

HD = 128
DOC_MAX = 256
EPS = 1e-05
ROPE_BASE = 500000.0


def from_behind(array, axis, by):
    length = lax.axis_size(axis)
    pairs = [(i, i + by) for i in range(length) if 0 <= i + by < length]
    return lax.ppermute(array, axis, pairs)


def rotate(packed, positions, head_count):
    row_count = packed.shape[0]
    head_width = packed.shape[1] // head_count
    half_width = head_width // 2
    frequency = jnp.power(
        ROPE_BASE, -jnp.arange(half_width, dtype=jnp.float32) * (2.0 / head_width)
    )
    angles = positions.astype(jnp.float32)[:, None] * frequency[None, :]
    cosine = jnp.cos(angles)[:, None, :]
    sine_part = jnp.sin(angles)[:, None, :]
    reshaped = packed.reshape(row_count, head_count, head_width)
    first_half = reshaped[:, :, :half_width]
    second = reshaped[:, :, half_width:]
    rotated = jnp.concatenate(
        [first_half * cosine - second * sine_part, second * cosine + first_half * sine_part], axis=2
    )
    return rotated.reshape(row_count, head_count * head_width)


def project(rows_in, norm_gain, w_query, w_key, w_value, positions):
    widened = rows_in.astype(jnp.float32)
    inverse_rms = lax.rsqrt(jnp.mean(widened * widened, axis=1, keepdims=True) + EPS)
    normed = (widened * inverse_rms * norm_gain[None, :]).astype(jnp.bfloat16)
    queries = jnp.dot(normed, w_query, preferred_element_type=jnp.float32)
    keys_f = jnp.dot(normed, w_key, preferred_element_type=jnp.float32)
    values_f = jnp.dot(normed, w_value, preferred_element_type=jnp.float32)
    queries = rotate(queries, positions, queries.shape[1] // HD).astype(jnp.bfloat16)
    keys_f = rotate(keys_f, positions, keys_f.shape[1] // HD).astype(jnp.bfloat16)
    return (queries, keys_f, values_f.astype(jnp.bfloat16))


def attend(
    queries, keys_in, values_in, query_doc, query_row, key_doc, key_row, key_live, offset, reach
):
    row_count = queries.shape[0]
    groups = keys_in.shape[1] // HD
    per_group = queries.shape[1] // keys_in.shape[1]
    window = row_count + reach

    def one_tile(index):
        first = index * row_count
        key_first = first + offset - reach
        near_keys = lax.dynamic_slice_in_dim(keys_in, key_first, window, 0)
        near_values = lax.dynamic_slice_in_dim(values_in, key_first, window, 0)
        near_doc = lax.dynamic_slice_in_dim(key_doc, key_first, window, 0)
        near_row = lax.dynamic_slice_in_dim(key_row, key_first, window, 0)
        near_live = lax.dynamic_slice_in_dim(key_live, key_first, window, 0)
        query_four = queries.reshape(row_count, groups, per_group, HD)
        key_three = near_keys.reshape(window, groups, HD)
        value_three = near_values.reshape(window, groups, HD)
        scores = jnp.einsum(
            "rgjd,kgd->gjrk", query_four, key_three, preferred_element_type=jnp.float32
        ) * HD ** (-0.5)
        allowed = (
            (query_doc[:, None] == near_doc[None, :])
            & (near_row[None, :] <= query_row[:, None])
            & (near_live[None, :] > 0)
        )
        allowed = allowed | (jnp.arange(window)[None, :] == jnp.arange(row_count)[:, None] + reach)
        scores = jnp.where(allowed[None, None], scores, -jnp.inf)
        highest = jnp.max(scores, axis=3, keepdims=True)
        weights = jnp.exp(scores - highest)
        weights = (weights / jnp.sum(weights, axis=3, keepdims=True)).astype(jnp.bfloat16)
        blended = jnp.einsum(
            "gjrk,kgd->rgjd", weights, value_three, preferred_element_type=jnp.float32
        )
        return blended.astype(jnp.bfloat16).reshape(row_count, groups * per_group * HD)

    tiles = lax.map(one_tile, jnp.arange(row_count // row_count, dtype=jnp.int32))
    return tiles.reshape(row_count, queries.shape[1])


def shards(hidden, norm_gain, w_query, w_key, w_value, doc_start, block_owner):
    home_hidden = lax.all_gather(hidden, "tp", axis=0, tiled=True)
    my_index = lax.axis_index("seq")
    home_rows = home_hidden.shape[0]
    home_blocks = block_owner.shape[0]
    block_rows = home_rows // home_blocks
    spill_rows = home_blocks // 4 * block_rows
    frame_size = home_rows + 2 * spill_rows
    all_rows = lax.axis_size("seq") * home_rows
    row_number = my_index * home_rows + jnp.arange(home_rows, dtype=jnp.int32)
    row_owner = jnp.repeat(block_owner, block_rows)
    frame_number = my_index * home_rows - spill_rows + jnp.arange(frame_size, dtype=jnp.int32)
    queries, keys_own, values_own = project(
        home_hidden, norm_gain, w_query, w_key, w_value, row_number - doc_start
    )
    left = from_behind((keys_own, values_own, doc_start), "seq", 1)
    left_live = jnp.ones((home_rows,), jnp.int32) * (my_index > 0).astype(jnp.int32)
    home_context = attend(
        queries,
        jnp.concatenate([left[0], keys_own], axis=0),
        jnp.concatenate([left[1], values_own], axis=0),
        doc_start,
        row_number,
        jnp.concatenate([left[2], doc_start], axis=0),
        jnp.concatenate([row_number - home_rows, row_number], axis=0),
        jnp.concatenate([left_live, jnp.ones((home_rows,), jnp.int32)], axis=0),
        home_rows,
        DOC_MAX,
    )
    arrived = []
    for direction in (1, -1):
        low_row = home_rows - spill_rows if direction == 1 else 0
        payload = (
            keys_own[low_row : low_row + spill_rows],
            values_own[low_row : low_row + spill_rows],
            row_owner[low_row : low_row + spill_rows],
        )
        arrived.append(from_behind((payload[0], payload[1], payload[2]), "seq", direction))
    from_left, from_right = arrived
    frame_keys = jnp.concatenate([from_left[0], keys_own, from_right[0]], axis=0)
    frame_values = jnp.concatenate([from_left[1], values_own, from_right[1]], axis=0)
    frame_owner = jnp.concatenate([from_left[2], row_owner, from_right[2]], axis=0)
    frame_live = (
        (frame_owner == my_index) & (frame_number >= 0) & (frame_number < all_rows)
    ).astype(jnp.int32)
    live_column = frame_live[:, None] > 0
    key_cache = jnp.where(live_column, frame_keys, jnp.zeros((), jnp.bfloat16))
    value_cache = jnp.where(live_column, frame_values, jnp.zeros((), jnp.bfloat16))
    context_rows = lax.all_to_all(home_context, "tp", split_axis=0, concat_axis=1, tiled=True)
    return (context_rows, key_cache, value_cache)


def solution(mesh):
    return jax.shard_map(
        shards,
        mesh=mesh,
        in_specs=(
            P(("seq", "tp"), None),
            P(),
            P(None, "tp"),
            P(None, "tp"),
            P(None, "tp"),
            P("seq"),
            P("seq"),
        ),
        out_specs=(P(("seq", "tp"), None), P("seq", "tp"), P("seq", "tp")),
        check_vma=False,
    )
```

profile of v0, /device:TPU:128, one launch (start us, length us, event | category | flops | bytes accessed | tf_op | source)
XLA Modules:
  0.0 141.9 jit_solution(14735143676403520581)
XLA Ops:
  7.9 0.8 fusion.35
  8.9 3.6 %collective-permute-start.4 = (s32[128]{0:T(128)S(1)}, s32[128]{0:T(128)S(1)}, u32[]{:S(2)}, u32[]{:S(2)}) collective-permute-start(s32[128]{0:T(128)S(1)} %slice.56), channel_id=1, source_target_pairs={{4,0},{8,4},{12,8},{16,12},{20,16},{24,20},{28,24},{32,28},{36,32}... | collective-permute-start | bytes 1544 | tf_op jit(solution)/shard_map/ppermute | solution.py:15
  12.7 1.9 %collective-permute-start.3 = (s32[128]{0:T(128)S(1)}, s32[128]{0:T(128)S(1)}, u32[]{:S(2)}, u32[]{:S(2)}) collective-permute-start(s32[128]{0:T(128)S(1)} %slice.54), channel_id=1, source_target_pairs={{0,4},{4,8},{8,12},{12,16},{16,20},{20,24},{24,28},{28,32},{32,36}... | collective-permute-start | bytes 1544 | tf_op jit(solution)/shard_map/ppermute | solution.py:15
  14.6 1.9 %collective-permute-start.1 = (s32[512]{0:T(512)}, s32[512]{0:T(512)S(1)}, u32[]{:S(2)}, u32[]{:S(2)}) collective-permute-start(s32[512]{0:T(512)} %param.12), channel_id=1, source_target_pairs={{0,4},{4,8},{8,12},{12,16},{16,20},{20,24},{24,28},{28,32},{32,36}... | collective-permute-start | bytes 6152 | tf_op jit(solution)/shard_map/ppermute | solution.py:15
  17.9 0.7 broadcast_in_dim.78
  18.7 0.8 copy.30
  19.5 0.8 copy.32
  20.9 2.1 %collective-permute-done.1 = s32[512]{0:T(512)S(1)} collective-permute-done((s32[512]{0:T(512)}, s32[512]{0:T(512)S(1)}, u32[]{:S(2)}, u32[]{:S(2)}) %collective-permute-start.1) | collective-permute-done | bytes 2080 | tf_op jit(solution)/shard_map/ppermute | solution.py:15
  23.8 2.2 %fusion.9 = pred[512,768]{0,1:T(8,128)(4,1)} fusion(s32[512]{0:T(512)S(1)} %iota_add_fusion.1, s32[512]{0:T(512)S(1)} %get-tuple-element.62, s32[512]{0:T(512)} %param.12, s32[768]{0:T(1024)S(1)} %dynamic_slice.25, s32[768]{0:T(1024)S(1)} %dynamic_slice.24, pred[768]{0:T(1024)(128)(4,1)S(1)} %slice_compare_fusion), kind=kLoop, calls=%fused_computation.15 | loop fusion | flops 2359296 | bytes 406272 | tf_op jit(solution)/shard_map/while/body/eval_jaxpr/or | solution.py:76
  25.9 36.2 %all-gather.2.cloned.1.call-done = bf16[512,4096]{1,0:T(8,128)(2,1)} async-done(((bf16[128,4096]{1,0:T(8,128)(2,1)}), bf16[512,4096]{1,0:T(8,128)(2,1)}) %all-gather.2.cloned.1.call-update) | async-done | bytes 4194320 | tf_op jit(solution)/shard_map/all_gather | solution.py:91
  62.1 3.2 %fusion.1 = f32[512]{0:T(512)S(1)} fusion(bf16[512,4096]{1,0:T(8,128)(2,1)} %all-gather.2.cloned.1.call-done), kind=kLoop, calls=%fused_computation.3 | loop fusion | flops 6290944 | bytes 4196352 | tf_op jit(solution)/shard_map/reduce_sum | solution.py:39
  65.6 2.0 %convolution_convert_fusion = bf16[512,256]{1,0:T(8,128)(2,1)} fusion(bf16[4096,256]{1,0:T(8,128)(2,1)S(1)} %copy-done, bf16[512,4096]{1,0:T(8,128)(2,1)S(1)} %copy-done.1, f32[4096]{0:T(1024)S(1)} %copy-done.4, f32[512]{0:T(512)S(1)} %add_rsqrt_fusion), kind=kOutput, calls=%fused_computation.18 | convolution fusion | flops 1082261504 | bytes 6572032 | tf_op jit(solution)/shard_map/dot_general | solution.py:43
  67.6 0.9 fusion.34
  68.5 1.9 %collective-permute-start = (bf16[512,256]{1,0:T(8,128)(2,1)}, bf16[512,256]{1,0:T(8,128)(2,1)}, u32[]{:S(2)}, u32[]{:S(2)}) collective-permute-start(bf16[512,256]{1,0:T(8,128)(2,1)} %convolution_convert_fusion), channel_id=1, source_target_pairs={{0,4},{4,8},{8,12},{12,16},{16,20},{20,24},{24,28},{28,32},{32,36}... | collective-permute-start | bytes 786440 | tf_op jit(solution)/shard_map/ppermute | solution.py:15
  70.5 3.5 %collective-permute-start.7 = (bf16[128,256]{1,0:T(8,128)(2,1)S(1)}, bf16[128,256]{1,0:T(8,128)(2,1)}, u32[]{:S(2)}, u32[]{:S(2)}) collective-permute-start(bf16[128,256]{1,0:T(8,128)(2,1)S(1)} %get-tuple-element.49), channel_id=1, source_target_pairs={{0,4},{4,8},{8,12},{12,16},{16,20},{20,24},{24,28},{28,32},{32,36}... | collective-permute-start | bytes 196616 | tf_op jit(solution)/shard_map/ppermute | solution.py:15
  73.9 5.4 %collective-permute-start.8 = (bf16[128,256]{1,0:T(8,128)(2,1)S(1)}, bf16[128,256]{1,0:T(8,128)(2,1)}, u32[]{:S(2)}, u32[]{:S(2)}) collective-permute-start(bf16[128,256]{1,0:T(8,128)(2,1)S(1)} %get-tuple-element.50), channel_id=1, source_target_pairs={{4,0},{8,4},{12,8},{16,12},{20,16},{24,20},{28,24},{32,28},{36,32}... | collective-permute-start | bytes 196616 | tf_op jit(solution)/shard_map/ppermute | solution.py:15
  79.4 1.6 %fusion.30 = f32[512,256]{0,1:T(8,128)S(1)} fusion(bf16[4096,256]{1,0:T(8,128)(2,1)S(1)} %copy-done.3, bf16[512,4096]{1,0:T(8,128)(2,1)S(1)} %copy-done.1, f32[4096]{0:T(1024)S(1)} %copy-done.4, f32[512]{0:T(512)S(1)} %add_rsqrt_fusion), kind=kOutput, calls=%fused_computation.59 | convolution fusion | flops 1082130432 | bytes 6834176 | tf_op jit(solution)/shard_map/dot_general | solution.py:42
  81.0 0.8 fusion.33
  82.0 1.2 copy.45
  83.2 1.6 %subtract_convert_fusion.1 = (bf16[512,2,64]{2,1,0:T(2,128)(2,1)S(1)}, bf16[512,2,64]{2,1,0:T(2,128)(2,1)S(1)}) fusion(f32[512,2,64]{2,1,0:T(2,128)S(1)} %copy.46, f32[512,2,64]{2,1,0:T(2,128)S(1)} %copy.45, f32[512,64]{1,0:T(8,128)} %copy.32, f32[512,64]{1,0:T(8,128)} %copy.30), kind=kLoop, calls=%fused_computation.24 | loop fusion | flops 524288 | bytes 1048576 | tf_op jit(solution)/shard_map/convert.2
  84.7 0.7 pad_maximum_fusion.3
  85.5 1.9 %collective-permute-start.2 = (bf16[512,256]{1,0:T(8,128)(2,1)S(1)}, bf16[512,256]{1,0:T(8,128)(2,1)S(1)}, u32[]{:S(2)}, u32[]{:S(2)}) collective-permute-start(bf16[512,256]{1,0:T(8,128)(2,1)S(1)} %bitcast.51), channel_id=1, source_target_pairs={{0,4},{4,8},{8,12},{12,16},{16,20},{20,24},{24,28},{28,32},{32,36}... | collective-permute-start | bytes 786440 | tf_op jit(solution)/shard_map/ppermute | solution.py:15
  87.4 5.9 %fusion.28 = f32[512,512]{0,1:T(8,128)S(1)} fusion(bf16[4096,512]{1,0:T(8,128)(2,1)} %param.9, bf16[512,4096]{1,0:T(8,128)(2,1)} %all-gather.2.cloned.1.call-done, f32[4096]{0:T(1024)} %param.8, f32[512]{0:T(512)S(1)} %add_rsqrt_fusion), kind=kOutput, calls=%fused_computation.58 | convolution fusion | flops 2155872256 | bytes 9455616 | tf_op jit(solution)/shard_map/dot_general | solution.py:41
  94.0 7.0 %collective-permute-start.6 = (bf16[128,256]{1,0:T(8,128)(2,1)S(1)}, bf16[128,256]{1,0:T(8,128)(2,1)S(1)}, u32[]{:S(2)}, u32[]{:S(2)}) collective-permute-start(bf16[128,256]{1,0:T(8,128)(2,1)S(1)} %bitcast.60), channel_id=1, source_target_pairs={{4,0},{8,4},{12,8},{16,12},{20,16},{24,20},{28,24},{32,28},{36,32}... | collective-permute-start | bytes 196616 | tf_op jit(solution)/shard_map/ppermute | solution.py:15
  100.9 2.1 %collective-permute-start.5 = (bf16[128,256]{1,0:T(8,128)(2,1)S(1)}, bf16[128,256]{1,0:T(8,128)(2,1)S(1)}, u32[]{:S(2)}, u32[]{:S(2)}) collective-permute-start(bf16[128,256]{1,0:T(8,128)(2,1)S(1)} %bitcast.59), channel_id=1, source_target_pairs={{0,4},{4,8},{8,12},{12,16},{16,20},{20,24},{24,28},{28,32},{32,36}... | collective-permute-start | bytes 196616 | tf_op jit(solution)/shard_map/ppermute | solution.py:15
  103.1 6.7 %collective-permute-done.5 = bf16[128,256]{1,0:T(8,128)(2,1)S(1)} collective-permute-done((bf16[128,256]{1,0:T(8,128)(2,1)S(1)}, bf16[128,256]{1,0:T(8,128)(2,1)S(1)}, u32[]{:S(2)}, u32[]{:S(2)}) %collective-permute-start.5) | collective-permute-done | bytes 65568 | tf_op jit(solution)/shard_map/ppermute | solution.py:15
  109.9 2.3 %maximum_select_fusion.1 = (bf16[768,256]{1,0:T(8,128)(2,1)}, bf16[768,256]{1,0:T(8,128)(2,1)S(1)}, bf16[768,256]{1,0:T(8,128)(2,1)S(1)}, bf16[768,256]{1,0:T(8,128)(2,1)}) fusion(bf16[128,256]{1,0:T(8,128)(2,1)} %collective-permute-done.8, bf16[512,256]{1,0:T(8,128)(2,1)} %convolution_convert_fusion, bf16[128,256]{1,0:T(8,128)(2,1)} %collective-permute-done.7, ...), kind=kLoop, calls=%fused_computation.28 | loop fusion | flops 4325376 | bytes 2884352 | tf_op jit(solution)/shard_map/jit(_where)/select_n | solution.py:137
  112.1 0.9 copy.42
  113.2 6.1 %fusion.36 = (f32[2,2,512]{2,1,0:T(2,128)S(1)}, f32[2,2,512,768]{2,3,1,0:T(8,128)}) fusion(pred[512,768]{0,1:T(8,128)(4,1)} %fusion.9, bf16[512,2,2,128]{0,3,2,1:T(8,128)(2,1)S(1)} %bitcast.53, bf16[768,2,128,1]{2,1,0,3:T(2,128)(2,1)S(1)} %bitcast.56), kind=kOutput, calls=%fused_computation.63 | convolution fusion | flops 408945408 | bytes 7610368 | tf_op jit(solution)/shard_map/while/body/eval_jaxpr/sub | solution.py:79
  119.3 3.4 %fusion.11 = bf16[512,2,2,128]{0,3,2,1:T(8,128)(2,1)S(1)} fusion(bf16[768,2,128,1]{0,2,3,1:T(8,128)(2,1)S(1)} %bitcast.55, f32[2,2,512,768]{2,3,1,0:T(8,128)} %get-tuple-element.60, f32[2,2,512]{2,1,0:T(2,128)S(1)} %get-tuple-element.59), kind=kOutput, calls=%fused_computation.17 | convolution fusion | flops 406061056 | bytes 7217152 | tf_op jit(solution)/shard_map/while/body/eval_jaxpr/gjrk,kgd->rgjd/dot_general | solution.py:81
  122.9 11.2 %all_to_all.19 = bf16[4,128,512]{1,2,0:T(8,128)(2,1)S(1)} all-to-all(bf16[4,128,512]{1,2,0:T(8,128)(2,1)S(1)} %copy.37), channel_id=1, replica_groups=mesh['seq'=64,'tp'=4] {'tp'}, dimensions={0} | all-to-all | bytes 1048576 | tf_op jit(solution)/shard_map/all_to_all | solution.py:138
  134.1 1.0 copy.38
  (47 shorter events, 5.0 us)
Async XLA Ops:
  7.2 58.2 %copy-start = (bf16[4096,256]{1,0:T(8,128)(2,1)S(1)}, bf16[4096,256]{1,0:T(8,128)(2,1)}, u32[]{:S(2)}) copy-start(bf16[4096,256]{1,0:T(8,128)(2,1)} %param.11) | copy-start | bytes 6291460
  7.2 58.2 %copy-start.4 = (f32[4096]{0:T(1024)S(1)}, f32[4096]{0:T(1024)}, u32[]{:S(2)}) copy-start(f32[4096]{0:T(1024)} %param.8) | copy-start | bytes 49156
  7.2 54.9 %all-gather.2.cloned.1.call-start = ((), (), s32[]{:S(2)}) async-start(), calls=%async_computation.1 | async-start | bytes 5242880 | tf_op jit(solution)/shard_map/all_gather | solution.py:91
  8.9 11.4 %collective-permute-start.4 = (s32[128]{0:T(128)S(1)}, s32[128]{0:T(128)S(1)}, u32[]{:S(2)}, u32[]{:S(2)}) collective-permute-start(s32[128]{0:T(128)S(1)} %slice.56), channel_id=1, source_target_pairs={{4,0},{8,4},{12,8},{16,12},{20,16},{24,20},{28,24},{32,28},{36,32}... | collective-permute-start | bytes 1544 | tf_op jit(solution)/shard_map/ppermute | solution.py:15
  12.7 8.2 %collective-permute-start.3 = (s32[128]{0:T(128)S(1)}, s32[128]{0:T(128)S(1)}, u32[]{:S(2)}, u32[]{:S(2)}) collective-permute-start(s32[128]{0:T(128)S(1)} %slice.54), channel_id=1, source_target_pairs={{0,4},{4,8},{8,12},{12,16},{16,20},{20,24},{24,28},{28,32},{32,36}... | collective-permute-start | bytes 1544 | tf_op jit(solution)/shard_map/ppermute | solution.py:15
  14.6 8.4 %collective-permute-start.1 = (s32[512]{0:T(512)}, s32[512]{0:T(512)S(1)}, u32[]{:S(2)}, u32[]{:S(2)}) collective-permute-start(s32[512]{0:T(512)} %param.12), channel_id=1, source_target_pairs={{0,4},{4,8},{8,12},{12,16},{16,20},{20,24},{24,28},{28,32},{32,36}... | collective-permute-start | bytes 6152 | tf_op jit(solution)/shard_map/ppermute | solution.py:15
  62.1 3.4 %copy-start.1 = (bf16[512,4096]{1,0:T(8,128)(2,1)S(1)}, bf16[512,4096]{1,0:T(8,128)(2,1)}, u32[]{:S(2)}) copy-start(bf16[512,4096]{1,0:T(8,128)(2,1)} %all-gather.2.cloned.1.call-done) | copy-start | bytes 12582916
  65.6 13.8 %copy-start.3 = (bf16[4096,256]{1,0:T(8,128)(2,1)S(1)}, bf16[4096,256]{1,0:T(8,128)(2,1)}, u32[]{:S(2)}) copy-start(bf16[4096,256]{1,0:T(8,128)(2,1)} %param.10) | copy-start | bytes 6291460
  68.5 41.3 %collective-permute-start = (bf16[512,256]{1,0:T(8,128)(2,1)}, bf16[512,256]{1,0:T(8,128)(2,1)}, u32[]{:S(2)}, u32[]{:S(2)}) collective-permute-start(bf16[512,256]{1,0:T(8,128)(2,1)} %convolution_convert_fusion), channel_id=1, source_target_pairs={{0,4},{4,8},{8,12},{12,16},{16,20},{20,24},{24,28},{28,32},{32,36}... | collective-permute-start | bytes 786440 | tf_op jit(solution)/shard_map/ppermute | solution.py:15
  70.5 30.5 %collective-permute-start.7 = (bf16[128,256]{1,0:T(8,128)(2,1)S(1)}, bf16[128,256]{1,0:T(8,128)(2,1)}, u32[]{:S(2)}, u32[]{:S(2)}) collective-permute-start(bf16[128,256]{1,0:T(8,128)(2,1)S(1)} %get-tuple-element.49), channel_id=1, source_target_pairs={{0,4},{4,8},{8,12},{12,16},{16,20},{20,24},{24,28},{28,32},{32,36}... | collective-permute-start | bytes 196616 | tf_op jit(solution)/shard_map/ppermute | solution.py:15
  73.9 29.2 %collective-permute-start.8 = (bf16[128,256]{1,0:T(8,128)(2,1)S(1)}, bf16[128,256]{1,0:T(8,128)(2,1)}, u32[]{:S(2)}, u32[]{:S(2)}) collective-permute-start(bf16[128,256]{1,0:T(8,128)(2,1)S(1)} %get-tuple-element.50), channel_id=1, source_target_pairs={{4,0},{8,4},{12,8},{16,12},{20,16},{24,20},{28,24},{32,28},{36,32}... | collective-permute-start | bytes 196616 | tf_op jit(solution)/shard_map/ppermute | solution.py:15
  85.5 24.4 %collective-permute-start.2 = (bf16[512,256]{1,0:T(8,128)(2,1)S(1)}, bf16[512,256]{1,0:T(8,128)(2,1)S(1)}, u32[]{:S(2)}, u32[]{:S(2)}) collective-permute-start(bf16[512,256]{1,0:T(8,128)(2,1)S(1)} %bitcast.51), channel_id=1, source_target_pairs={{0,4},{4,8},{8,12},{12,16},{16,20},{20,24},{24,28},{28,32},{32,36}... | collective-permute-start | bytes 786440 | tf_op jit(solution)/shard_map/ppermute | solution.py:15
  94.0 9.1 %collective-permute-start.6 = (bf16[128,256]{1,0:T(8,128)(2,1)S(1)}, bf16[128,256]{1,0:T(8,128)(2,1)S(1)}, u32[]{:S(2)}, u32[]{:S(2)}) collective-permute-start(bf16[128,256]{1,0:T(8,128)(2,1)S(1)} %bitcast.60), channel_id=1, source_target_pairs={{4,0},{8,4},{12,8},{16,12},{20,16},{24,20},{28,24},{32,28},{36,32}... | collective-permute-start | bytes 196616 | tf_op jit(solution)/shard_map/ppermute | solution.py:15
  100.9 8.9 %collective-permute-start.5 = (bf16[128,256]{1,0:T(8,128)(2,1)S(1)}, bf16[128,256]{1,0:T(8,128)(2,1)S(1)}, u32[]{:S(2)}, u32[]{:S(2)}) collective-permute-start(bf16[128,256]{1,0:T(8,128)(2,1)S(1)} %bitcast.59), channel_id=1, source_target_pairs={{0,4},{4,8},{8,12},{12,16},{16,20},{20,24},{24,28},{28,32},{32,36}... | collective-permute-start | bytes 196616 | tf_op jit(solution)/shard_map/ppermute | solution.py:15
  113.2 6.1 %copy-start.2 = (bf16[768,256]{0,1:T(8,128)(2,1)S(1)}, bf16[768,256]{0,1:T(8,128)(2,1)}, u32[]{:S(2)}) copy-start(bf16[768,256]{0,1:T(8,128)(2,1)} %copy.42) | copy-start | bytes 1179652
Sparse Core Ops, SparseCore 0:
  9.8 52.2 all-gather.1
where the time goes:
time: 143 us; the launch traced here: 142 us
  waiting for transfers between devices  46.3 us (32%)
  starting transfers between devices  29.3 us (20%)
  matrix products  19.1 us (13%)
  between operations  14.4 us (10%)
  other arithmetic  12.5 us (9%)
  blocking collectives  11.2 us (8%)
  local copies, waits for them, and re-layouts  9.14 us (6%)
    all_gather x1, waiting for transfers between devices, shards(): home_hidden = lax.all_gather(hidden, 'tp', axis=0, tiled=True)  36.2 us
    ppermute x9, starting transfers between devices, from_behind(): return lax.ppermute(array, axis, pairs)  29.3 us
    all_to_all x1, blocking collectives, shards(): lax.all_to_all(home_context, 'tp', split_axis=0, concat_axis=1, tiled=True)  11.2 us
    ppermute x9, waiting for transfers between devices, from_behind(): return lax.ppermute(array, axis, pairs)  9.44 us
    sub x1, matrix products, one_tile(): weights = jnp.exp(scores - highest)  6.09 us
    dot_general x1, matrix products, project(): queries = jnp.dot(normed, w_query, preferred_element_type=jnp.float32)  5.94 us
    dot_general x1, matrix products, one_tile(): jnp.einsum('gjrk,kgd->rgjd', weights, value_three, preferred_element_type...  3.37 us
    reduce_sum x1, other arithmetic, project(): jnp.mean(widened * widened, axis=1, keepdims=True) + EPS  3.23 us
  transfers between devices with their start and end apart: 10, of which 4 were waited for; matrix products, arithmetic and copies ran while one was open for 14% of the time, Pallas kernels for 0%

commit v1 on v0

--- a/solution.py
+++ b/solution.py
@@ -88,7 +88,9 @@
 
 
 def shards(hidden, norm_gain, w_query, w_key, w_value, doc_start, block_owner):
-    home_hidden = lax.all_gather(hidden, "tp", axis=0, tiled=True)
+    home_hidden = jnp.concatenate(
+        lax.all_to_all(jnp.stack([hidden] * lax.axis_size("tp")), "tp", 0, 0), axis=0
+    )
     my_index = lax.axis_index("seq")
     home_rows = home_hidden.shape[0]
     home_blocks = block_owner.shape[0]

time: 143 us -> 133 us (0.930)
  between operations: 14.4 us -> 1 us
  waiting for transfers between devices: 46.3 us -> 34.4 us
  local copies, waits for them, and re-layouts: 9.14 us -> 18 us
  starting transfers between devices: 29.3 us -> 34.2 us
  other arithmetic: 12.5 us -> 16.2 us
    all_gather x1 -> x0, waiting for transfers between devices: 36.2 us -> none  [shards(): home_hidden = lax.all_gather(hidden, 'tp', axis=0, tiled=True)]
    all_to_all x0 -> x1, waiting for transfers between devices: none -> 28.4 us  [shards(): lax.all_to_all(jnp.stack([hidden] * lax.axis_size('tp')), 'tp', 0, 0)]
    dot_general x0 -> x2, local copies, waits for them, and re-layouts: none -> 10.5 us  [the longest x1 6.39 us: project(): queries = jnp.dot(normed, w_query, preferred_element_type=jnp.float32)]
    convert_element_type x0 -> x2, other arithmetic: none -> 7.79 us  [project(): normed = (widened * inverse_rms * norm_gain[None, :]).astype(jnp.bfloat16)]
    all_to_all x0 -> x1, starting transfers between devices: none -> 4.97 us  [shards(): lax.all_to_all(jnp.stack([hidden] * lax.axis_size('tp')), 'tp', 0, 0)]
    another operation x0 -> x1, local copies, waits for them, and re-layouts: none -> 3.85 us  [shards(): jnp.stack([hidden] * lax.axis_size('tp'))]
    ppermute x9, waiting for transfers between devices: 9.44 us -> 5.98 us  [from_behind(): return lax.ppermute(array, axis, pairs)]
    another operation x2, other arithmetic: 1.76 us -> 0.27 us
  transfers between devices with their start and end apart: 10 -> 10, of which waited for: 4 -> 2; matrix products, arithmetic and copies ran while one was open for 14% -> 19% of each run, Pallas kernels for 0% -> 0%
where the time goes in v1:
time: 133 us; the launch traced here: 132 us
  waiting for transfers between devices  34.4 us (26%)
  starting transfers between devices  34.2 us (26%)
  local copies, waits for them, and re-layouts  18 us (14%)
  matrix products  17.9 us (13%)
  other arithmetic  16.2 us (12%)
  blocking collectives  10.5 us (8%)
    ppermute x9, starting transfers between devices, from_behind(): return lax.ppermute(array, axis, pairs)  29.3 us
    all_to_all x1, waiting for transfers between devices, shards(): lax.all_to_all(jnp.stack([hidden] * lax.axis_size('tp')), 'tp', 0, 0)  28.4 us
    all_to_all x1, blocking collectives, shards(): lax.all_to_all(home_context, 'tp', split_axis=0, concat_axis=1, tiled=True)  10.5 us
    convert_element_type x2, other arithmetic, project(): normed = (widened * inverse_rms * norm_gain[None, :]).astype(jnp.bfloat16)  7.79 us
    dot_general x1, local copies, waits for them, and re-layouts, project(): queries = jnp.dot(normed, w_query, preferred_element_type=jnp.float32)  6.39 us
    sub x1, matrix products, one_tile(): weights = jnp.exp(scores - highest)  6.17 us
    ppermute x9, waiting for transfers between devices, from_behind(): return lax.ppermute(array, axis, pairs)  5.98 us
    dot_general x1, matrix products, project(): queries = jnp.dot(normed, w_query, preferred_element_type=jnp.float32)  5.83 us
  transfers between devices with their start and end apart: 10, of which 2 were waited for; matrix products, arithmetic and copies ran while one was open for 19% of the time, Pallas kernels for 0%

profile of v1, /device:TPU:128, one launch (start us, length us, event | category | flops | bytes accessed | tf_op | source)
XLA Modules:
  0.0 132.2 jit_solution(12077392854586512323)
XLA Ops:
  0.6 3.8 %stack.2 = bf16[4,128,4096]{2,1,0:T(8,128)(2,1)} broadcast(bf16[128,4096]{1,0:T(8,128)(2,1)} %param.7), dimensions={1,2} | broadcast | bytes 5242880 | tf_op jit(solution)/shard_map/stack | solution.py:92
  4.5 5.0 %all-to-all-start = ((bf16[4,128,4096]{2,1,0:T(8,128)(2,1)}), bf16[4,128,4096]{2,1,0:T(8,128)(2,1)}, u32[]{:S(2)}, u32[]{:S(2)}) async-start(bf16[4,128,4096]{2,1,0:T(8,128)(2,1)} %stack.2), calls=%async_computation | async-start | bytes 8388608 | tf_op jit(solution)/shard_map/all_to_all | solution.py:92
  9.7 3.6 %collective-permute-start.4 = (s32[128]{0:T(128)S(1)}, s32[128]{0:T(128)S(1)}, u32[]{:S(2)}, u32[]{:S(2)}) collective-permute-start(s32[128]{0:T(128)S(1)} %slice.56), channel_id=1, source_target_pairs={{4,0},{8,4},{12,8},{16,12},{20,16},{24,20},{28,24},{32,28},{36,32}... | collective-permute-start | bytes 1544 | tf_op jit(solution)/shard_map/ppermute | solution.py:15
  13.5 1.9 %collective-permute-start.3 = (s32[128]{0:T(128)S(1)}, s32[128]{0:T(128)S(1)}, u32[]{:S(2)}, u32[]{:S(2)}) collective-permute-start(s32[128]{0:T(128)S(1)} %slice.54), channel_id=1, source_target_pairs={{0,4},{4,8},{8,12},{12,16},{16,20},{20,24},{24,28},{28,32},{32,36}... | collective-permute-start | bytes 1544 | tf_op jit(solution)/shard_map/ppermute | solution.py:15
  15.5 1.9 %collective-permute-start.1 = (s32[512]{0:T(512)S(1)}, s32[512]{0:T(512)S(1)}, u32[]{:S(2)}, u32[]{:S(2)}) collective-permute-start(s32[512]{0:T(512)S(1)} %copy-done.4), channel_id=1, source_target_pairs={{0,4},{4,8},{8,12},{12,16},{16,20},{20,24},{24,28},{28,32},{32,36}... | collective-permute-start | bytes 6152 | tf_op jit(solution)/shard_map/ppermute | solution.py:15
  17.5 0.5 multiply_cosine_fusion
  18.2 4.1 %copy.36 = bf16[256,4096]{1,0:T(8,128)(2,1)} copy(bf16[256,4096]{0,1:T(8,128)(2,1)} %bitcast.58) | data formatting | bytes 4194304 | tf_op jit(solution)/shard_map/dot_general | solution.py:42
  22.3 6.4 %copy.40 = bf16[512,4096]{1,0:T(8,128)(2,1)} copy(bf16[512,4096]{0,1:T(8,128)(2,1)} %bitcast.56) | data formatting | bytes 8388608 | tf_op jit(solution)/shard_map/dot_general | solution.py:41
  28.7 1.5 %fusion.8 = pred[512,768]{0,1:T(8,128)(4,1)} fusion(s32[512]{0:T(512)S(1)} %iota_add_fusion.1, s32[512]{0:T(512)S(1)} %get-tuple-element.59, s32[512]{0:T(512)S(1)} %copy-done.4, s32[768]{0:T(1024)S(1)} %dynamic_slice.25, s32[768]{0:T(1024)S(1)} %dynamic_slice.24, pred[768]{0:T(1024)(128)(4,1)S(1)} %slice_compare_fusion), kind=kLoop, calls=%fused_computation.15 | loop fusion | flops 2359296 | bytes 406272 | tf_op jit(solution)/shard_map/while/body/eval_jaxpr/or | solution.py:76
  30.2 28.4 %all-to-all-done = bf16[4,128,4096]{2,1,0:T(8,128)(2,1)} async-done(((bf16[4,128,4096]{2,1,0:T(8,128)(2,1)}), bf16[4,128,4096]{2,1,0:T(8,128)(2,1)}, u32[]{:S(2)}, u32[]{:S(2)}) %all-to-all-start) | async-done | bytes 4194336 | tf_op jit(solution)/shard_map/all_to_all | solution.py:92
  58.6 3.1 %multiply_reduce_fusion = f32[4,128]{1,0:T(4,128)S(1)} fusion(bf16[4,128,4096]{2,1,0:T(8,128)(2,1)} %all-to-all-done), kind=kLoop, calls=%fused_computation.5 | loop fusion | flops 6290944 | bytes 4196352 | tf_op jit(solution)/shard_map/reduce_sum | solution.py:39
  61.7 3.8 %fusion.2 = bf16[512,4096]{1,0:T(8,128)(2,1)S(1)} fusion(bf16[4,128,4096]{2,1,0:T(8,128)(2,1)} %all-to-all-done, f32[4096]{0:T(1024)S(1)} %copy-done.3, f32[512]{0:T(512)S(1)} %get-tuple-element.51), kind=kLoop, calls=%fused_computation.3 | loop fusion | flops 8388608 | bytes 8407040 | tf_op jit(solution)/shard_map/convert_element_type | solution.py:40
  65.6 1.3 convolution_convert_fusion
  66.8 0.7 fusion.30
  67.5 1.9 %collective-permute-start = (bf16[512,256]{1,0:T(8,128)(2,1)S(1)}, bf16[512,256]{1,0:T(8,128)(2,1)}, u32[]{:S(2)}, u32[]{:S(2)}) collective-permute-start(bf16[512,256]{1,0:T(8,128)(2,1)S(1)} %convolution_convert_fusion), channel_id=1, source_target_pairs={{0,4},{4,8},{8,12},{12,16},{16,20},{20,24},{24,28},{28,32},{32,36}... | collective-permute-start | bytes 786440 | tf_op jit(solution)/shard_map/ppermute | solution.py:15
  69.4 4.0 %multiply_convert_fusion = bf16[4,128,4096]{2,1,0:T(8,128)(2,1)S(1)} fusion(bf16[4,128,4096]{2,1,0:T(8,128)(2,1)} %all-to-all-done, f32[4096]{0:T(1024)S(1)} %copy-done.3, f32[4,128]{1,0:T(4,128)S(1)} %get-tuple-element.50), kind=kLoop, calls=%fused_computation.4 | loop fusion | flops 8388608 | bytes 8407040 | tf_op jit(solution)/shard_map/convert_element_type | solution.py:40
  73.4 1.3 fusion.37
  74.8 0.6 copy-done.1
  75.4 7.0 %collective-permute-start.8 = (bf16[128,256]{1,0:T(8,128)(2,1)}, bf16[128,256]{1,0:T(8,128)(2,1)}, u32[]{:S(2)}, u32[]{:S(2)}) collective-permute-start(bf16[128,256]{1,0:T(8,128)(2,1)} %get-tuple-element.43), channel_id=1, source_target_pairs={{4,0},{8,4},{12,8},{16,12},{20,16},{24,20},{28,24},{32,28},{36,32}... | collective-permute-start | bytes 196616 | tf_op jit(solution)/shard_map/ppermute | solution.py:15
  82.4 1.9 %collective-permute-start.7 = (bf16[128,256]{1,0:T(8,128)(2,1)}, bf16[128,256]{1,0:T(8,128)(2,1)}, u32[]{:S(2)}, u32[]{:S(2)}) collective-permute-start(bf16[128,256]{1,0:T(8,128)(2,1)} %get-tuple-element.42), channel_id=1, source_target_pairs={{0,4},{4,8},{8,12},{12,16},{16,20},{20,24},{24,28},{28,32},{32,36}... | collective-permute-start | bytes 196616 | tf_op jit(solution)/shard_map/ppermute | solution.py:15
  84.5 1.9 %collective-permute-start.2 = (bf16[512,256]{1,0:T(8,128)(2,1)S(1)}, bf16[512,256]{1,0:T(8,128)(2,1)}, u32[]{:S(2)}, u32[]{:S(2)}) collective-permute-start(bf16[512,256]{1,0:T(8,128)(2,1)S(1)} %copy.37), channel_id=1, source_target_pairs={{0,4},{4,8},{8,12},{12,16},{16,20},{20,24},{24,28},{28,32},{32,36}... | collective-permute-start | bytes 786440 | tf_op jit(solution)/shard_map/ppermute | solution.py:15
  86.5 7.0 %collective-permute-start.6 = (bf16[128,256]{1,0:T(8,128)(2,1)S(1)}, bf16[128,256]{1,0:T(8,128)(2,1)}, u32[]{:S(2)}, u32[]{:S(2)}) collective-permute-start(bf16[128,256]{1,0:T(8,128)(2,1)S(1)} %copy.42), channel_id=1, source_target_pairs={{4,0},{8,4},{12,8},{16,12},{20,16},{24,20},{28,24},{32,28},{36,32}... | collective-permute-start | bytes 196616 | tf_op jit(solution)/shard_map/ppermute | solution.py:15
  93.5 5.8 %fusion.38 = f32[512,4,128]{0,2,1:T(8,128)S(1)} fusion(bf16[512,4096,1]{1,0,2:T(8,128)(2,1)} %bitcast.55, bf16[4,128,4096]{2,1,0:T(8,128)(2,1)} %bitcast.57), kind=kOutput, calls=%fused_computation.64 | convolution fusion | flops 2147483648 | bytes 9437184 | tf_op jit(solution)/shard_map/dot_general | solution.py:41
  99.3 0.2 subtract_convert_fusion
  99.6 2.1 %collective-permute-start.5 = (bf16[128,256]{1,0:T(8,128)(2,1)S(1)}, bf16[128,256]{1,0:T(8,128)(2,1)S(1)}, u32[]{:S(2)}, u32[]{:S(2)}) collective-permute-start(bf16[128,256]{1,0:T(8,128)(2,1)S(1)} %copy.41), channel_id=1, source_target_pairs={{0,4},{4,8},{8,12},{12,16},{16,20},{20,24},{24,28},{28,32},{32,36}... | collective-permute-start | bytes 196616 | tf_op jit(solution)/shard_map/ppermute | solution.py:15
  101.7 0.8 pad_maximum_fusion
  102.6 6.0 %collective-permute-done.5 = bf16[128,256]{1,0:T(8,128)(2,1)S(1)} collective-permute-done((bf16[128,256]{1,0:T(8,128)(2,1)S(1)}, bf16[128,256]{1,0:T(8,128)(2,1)S(1)}, u32[]{:S(2)}, u32[]{:S(2)}) %collective-permute-start.5) | collective-permute-done | bytes 65568 | tf_op jit(solution)/shard_map/ppermute | solution.py:15
  108.5 2.2 %maximum_select_fusion.1 = (bf16[768,256]{1,0:T(8,128)(2,1)}, bf16[768,256]{1,0:T(8,128)(2,1)S(1)}, bf16[768,256]{1,0:T(8,128)(2,1)S(1)}, bf16[768,256]{1,0:T(8,128)(2,1)}) fusion(bf16[128,256]{1,0:T(8,128)(2,1)} %collective-permute-done.8, bf16[512,256]{1,0:T(8,128)(2,1)S(1)} %convolution_convert_fusion, bf16[128,256]{1,0:T(8,128)(2,1)} %collective-permute-done.7, ...), kind=kLoop, calls=%fused_computation.26 | loop fusion | flops 4325376 | bytes 2884352 | tf_op jit(solution)/shard_map/jit(_where)/select_n | solution.py:139
  111.0 6.2 %fusion.32 = (f32[2,2,512]{2,1,0:T(2,128)S(1)}, f32[2,2,512,768]{2,3,1,0:T(8,128)}) fusion(pred[512,768]{0,1:T(8,128)(4,1)} %fusion.8, bf16[512,2,2,128]{0,3,2,1:T(8,128)(2,1)} %bitcast.62, bf16[768,2,128,1]{2,1,0,3:T(2,128)(2,1)S(1)} %bitcast.64), kind=kOutput, calls=%fused_computation.62 | convolution fusion | flops 408945408 | bytes 7610368 | tf_op jit(solution)/shard_map/while/body/eval_jaxpr/sub | solution.py:79
  117.1 3.4 %fusion.10 = bf16[512,2,2,128]{0,3,2,1:T(8,128)(2,1)S(1)} fusion(bf16[768,2,128,1]{0,2,3,1:T(8,128)(2,1)S(1)} %bitcast.63, f32[2,2,512,768]{2,3,1,0:T(8,128)} %get-tuple-element.57, f32[2,2,512]{2,1,0:T(2,128)S(1)} %get-tuple-element.56), kind=kOutput, calls=%fused_computation.17 | convolution fusion | flops 406061056 | bytes 7217152 | tf_op jit(solution)/shard_map/while/body/eval_jaxpr/gjrk,kgd->rgjd/dot_general | solution.py:81
  120.7 10.5 %all_to_all.24 = bf16[4,128,512]{1,2,0:T(8,128)(2,1)S(1)} all-to-all(bf16[4,128,512]{1,2,0:T(8,128)(2,1)S(1)} %copy.27), channel_id=1, replica_groups=mesh['seq'=64,'tp'=4] {'tp'}, dimensions={0} | all-to-all | bytes 1048576 | tf_op jit(solution)/shard_map/all_to_all | solution.py:140
  131.2 1.0 copy.30
  (48 shorter events, 1.6 us)
Async XLA Ops:
  0.6 64.9 %copy-start = (bf16[4096,256]{1,0:T(8,128)(2,1)S(1)}, bf16[4096,256]{1,0:T(8,128)(2,1)}, u32[]{:S(2)}) copy-start(bf16[4096,256]{1,0:T(8,128)(2,1)} %param.11) | copy-start | bytes 6291460
  4.5 5.0 %copy-start.5 = (s32[16]{0:T(128)S(1)}, s32[16]{0:T(128)}, u32[]{:S(2)}) copy-start(s32[16]{0:T(128)} %param.13) | copy-start | bytes 196
  4.5 10.9 %copy-start.4 = (s32[512]{0:T(512)S(1)}, s32[512]{0:T(512)}, u32[]{:S(2)}) copy-start(s32[512]{0:T(512)} %param.12) | copy-start | bytes 6148
  4.5 54.1 %all-to-all-start = ((bf16[4,128,4096]{2,1,0:T(8,128)(2,1)}), bf16[4,128,4096]{2,1,0:T(8,128)(2,1)}, u32[]{:S(2)}, u32[]{:S(2)}) async-start(bf16[4,128,4096]{2,1,0:T(8,128)(2,1)} %stack.2), calls=%async_computation | async-start | bytes 8388608 | tf_op jit(solution)/shard_map/all_to_all | solution.py:92
  9.7 19.0 %collective-permute-start.4 = (s32[128]{0:T(128)S(1)}, s32[128]{0:T(128)S(1)}, u32[]{:S(2)}, u32[]{:S(2)}) collective-permute-start(s32[128]{0:T(128)S(1)} %slice.56), channel_id=1, source_target_pairs={{4,0},{8,4},{12,8},{16,12},{20,16},{24,20},{28,24},{32,28},{36,32}... | collective-permute-start | bytes 1544 | tf_op jit(solution)/shard_map/ppermute | solution.py:15
  13.5 15.2 %collective-permute-start.3 = (s32[128]{0:T(128)S(1)}, s32[128]{0:T(128)S(1)}, u32[]{:S(2)}, u32[]{:S(2)}) collective-permute-start(s32[128]{0:T(128)S(1)} %slice.54), channel_id=1, source_target_pairs={{0,4},{4,8},{8,12},{12,16},{16,20},{20,24},{24,28},{28,32},{32,36}... | collective-permute-start | bytes 1544 | tf_op jit(solution)/shard_map/ppermute | solution.py:15
  15.5 13.3 %collective-permute-start.1 = (s32[512]{0:T(512)S(1)}, s32[512]{0:T(512)S(1)}, u32[]{:S(2)}, u32[]{:S(2)}) collective-permute-start(s32[512]{0:T(512)S(1)} %copy-done.4), channel_id=1, source_target_pairs={{0,4},{4,8},{8,12},{12,16},{16,20},{20,24},{24,28},{28,32},{32,36}... | collective-permute-start | bytes 6152 | tf_op jit(solution)/shard_map/ppermute | solution.py:15
  28.7 33.0 %copy-start.3 = (f32[4096]{0:T(1024)S(1)}, f32[4096]{0:T(1024)}, u32[]{:S(2)}) copy-start(f32[4096]{0:T(1024)} %param.8) | copy-start | bytes 49156
  67.5 41.1 %collective-permute-start = (bf16[512,256]{1,0:T(8,128)(2,1)S(1)}, bf16[512,256]{1,0:T(8,128)(2,1)}, u32[]{:S(2)}, u32[]{:S(2)}) collective-permute-start(bf16[512,256]{1,0:T(8,128)(2,1)S(1)} %convolution_convert_fusion), channel_id=1, source_target_pairs={{0,4},{4,8},{8,12},{12,16},{16,20},{20,24},{24,28},{28,32},{32,36}... | collective-permute-start | bytes 786440 | tf_op jit(solution)/shard_map/ppermute | solution.py:15
  69.4 4.0 %copy-start.2 = (bf16[256,4096]{1,0:T(8,128)(2,1)S(1)}, bf16[256,4096]{1,0:T(8,128)(2,1)}, u32[]{:S(2)}) copy-start(bf16[256,4096]{1,0:T(8,128)(2,1)} %copy.36) | copy-start | bytes 6291460
  73.4 2.0 %copy-start.1 = (bf16[4,128,4096]{2,1,0:T(8,128)(2,1)}, bf16[4,128,4096]{2,1,0:T(8,128)(2,1)S(1)}, u32[]{:S(2)}) copy-start(bf16[4,128,4096]{2,1,0:T(8,128)(2,1)S(1)} %multiply_convert_fusion) | copy-start | bytes 12582916
  75.4 24.2 %collective-permute-start.8 = (bf16[128,256]{1,0:T(8,128)(2,1)}, bf16[128,256]{1,0:T(8,128)(2,1)}, u32[]{:S(2)}, u32[]{:S(2)}) collective-permute-start(bf16[128,256]{1,0:T(8,128)(2,1)} %get-tuple-element.43), channel_id=1, source_target_pairs={{4,0},{8,4},{12,8},{16,12},{20,16},{24,20},{28,24},{32,28},{36,32}... | collective-permute-start | bytes 196616 | tf_op jit(solution)/shard_map/ppermute | solution.py:15
  82.4 20.2 %collective-permute-start.7 = (bf16[128,256]{1,0:T(8,128)(2,1)}, bf16[128,256]{1,0:T(8,128)(2,1)}, u32[]{:S(2)}, u32[]{:S(2)}) collective-permute-start(bf16[128,256]{1,0:T(8,128)(2,1)} %get-tuple-element.42), channel_id=1, source_target_pairs={{0,4},{4,8},{8,12},{12,16},{16,20},{20,24},{24,28},{28,32},{32,36}... | collective-permute-start | bytes 196616 | tf_op jit(solution)/shard_map/ppermute | solution.py:15
  84.5 24.1 %collective-permute-start.2 = (bf16[512,256]{1,0:T(8,128)(2,1)S(1)}, bf16[512,256]{1,0:T(8,128)(2,1)}, u32[]{:S(2)}, u32[]{:S(2)}) collective-permute-start(bf16[512,256]{1,0:T(8,128)(2,1)S(1)} %copy.37), channel_id=1, source_target_pairs={{0,4},{4,8},{8,12},{12,16},{16,20},{20,24},{24,28},{28,32},{32,36}... | collective-permute-start | bytes 786440 | tf_op jit(solution)/shard_map/ppermute | solution.py:15
  86.5 16.1 %collective-permute-start.6 = (bf16[128,256]{1,0:T(8,128)(2,1)S(1)}, bf16[128,256]{1,0:T(8,128)(2,1)}, u32[]{:S(2)}, u32[]{:S(2)}) collective-permute-start(bf16[128,256]{1,0:T(8,128)(2,1)S(1)} %copy.42), channel_id=1, source_target_pairs={{4,0},{8,4},{12,8},{16,12},{20,16},{24,20},{28,24},{32,28},{36,32}... | collective-permute-start | bytes 196616 | tf_op jit(solution)/shard_map/ppermute | solution.py:15
  99.6 8.9 %collective-permute-start.5 = (bf16[128,256]{1,0:T(8,128)(2,1)S(1)}, bf16[128,256]{1,0:T(8,128)(2,1)S(1)}, u32[]{:S(2)}, u32[]{:S(2)}) collective-permute-start(bf16[128,256]{1,0:T(8,128)(2,1)S(1)} %copy.41), channel_id=1, source_target_pairs={{0,4},{4,8},{8,12},{12,16},{16,20},{20,24},{24,28},{28,32},{32,36}... | collective-permute-start | bytes 196616 | tf_op jit(solution)/shard_map/ppermute | solution.py:15
